TPU v7x, 128 devices: a whole 4x4x4 slice. The times are simulated.
128 devices in a mesh: row: 16 (over y_hi, x, core), col: 8 (over y_lo, z).
Axes of the slice: x: 4, y: 4 (y_hi: 2, y_lo: 2; y = y_hi * 2 + y_lo), z: 4, core: 2. Of those that a mesh axis runs over, the one named last changes fastest.
Arguments:
- pair_feature_map: bfloat16 [64, 1024, 1024], P(None, 'row', 'col'), may hold values from -6 to 6
- conv_weight: bfloat16 [3, 3, 64, 64], replicated, may hold values from -0.25 to 0.25
- conv_bias: float32 [64], replicated, may hold values from -3 to 3
- cotangent: bfloat16 [64, 1024, 1024], P(None, 'row', 'col'), may hold values from -6 to 6
Outputs:
- symmetric: bfloat16 [64, 1024, 1024], P(None, 'row', 'col')
- grad_input: bfloat16 [64, 1024, 1024], P(None, 'row', 'col')
- grad_weight: float32 [3, 3, 64, 64], replicated
- grad_bias: float32 [64], replicated
All inputs are finite; a program needn't handle non-finite values.
Results may differ from a plain program's by a relative error of at most 0.0085.
Values may be sent and summed in bfloat16 or wider, within the bound.
A program may use at most 128 MiB of HBM per device.

v0:
```python
import functools

import jax
import jax.numpy as jnp
from jax import lax
from jax.experimental import pallas as pl
from jax.experimental.pallas import tpu as pltpu
from jax.sharding import PartitionSpec as P

MESH = pl.DeviceIdType.MESH
F32 = jnp.float32
BF16 = jnp.bfloat16

C = 64
R = 64
W = 128
D = 8
PIECES = 32


def position():
    return lax.axis_index("row"), lax.axis_index("col")


def mod4(n):
    return lax.rem(n, 4)


def swap_middle(y):
    return jnp.where(jnp.logical_or(y == 1, y == 2), 3 - y, y)


def swap_outer(y):
    return jnp.where(jnp.logical_or(y == 0, y == 3), 3 - y, y)


def next_stop(stage, p):
    mode, n = p
    r, c = position()
    chip_row, core = lax.div(r, 2), lax.rem(r, 2)
    x, z = mod4(chip_row), mod4(c)
    y = 2 * lax.div(chip_row, 4) + lax.div(c, 4)
    j, how = mod4(n), lax.div(n, 4)
    u, v = (z, x) if mode else (x, z)
    if stage == 0:
        u = mod4(u + v + j)
    elif stage == 1:
        v = mod4(u - j - v + 8)
    else:
        u = mod4(u - v - j + 8)
    nx, nz = (v, u) if mode else (u, v)
    around = swap_outer(y) if stage == 1 else y + 1 - 2 * lax.rem(y, 2)
    ny = jnp.where(how == 3, around, jnp.where(how == stage, swap_middle(y), y))
    nr = lax.div(ny, 2) * 8 + nx * 2 + core
    nc = lax.rem(ny, 2) * 4 + nz
    return nr, nc, jnp.logical_and(nr == r, nc == c)


def relay_copy(stops, s, p, sems):
    nr, nc, here = next_stop(s, p)
    mode, n = p
    i = 2 * n + mode
    ssem, rsem = sems
    remote = lambda: pltpu.make_async_remote_copy(
        stops[s].at[i], stops[s + 1].at[i], ssem.at[s, i], rsem.at[s, i],
        device_id=(nr, nc), device_id_type=MESH)
    local = lambda: pltpu.make_async_copy(stops[s].at[i], stops[s + 1].at[i], rsem.at[s, i])
    return remote, local, here


def relay_start(stops, s, p, sems):
    remote, local, here = relay_copy(stops, s, p, sems)

    @pl.when(here)
    def _():
        local().start()

    @pl.when(jnp.logical_not(here))
    def _():
        remote().start()


def relay_arrived(stops, s, p, sems):
    i = 2 * p[1] + p[0]
    pltpu.make_async_copy(stops[s].at[i], stops[s + 1].at[i], sems[1].at[s, i]).wait()


def relay_sent(stops, s, p, sems):
    remote, _, here = relay_copy(stops, s, p, sems)

    @pl.when(jnp.logical_not(here))
    def _():
        remote().wait_send()


def pass_on(stops, s, n, sems):
    for mode in range(2):
        relay_arrived(stops, s, (mode, n), sems)
        relay_start(stops, s + 1, (mode, n), sems)


def loop(n, body):
    def step(i, carry):
        body(i)
        return carry

    lax.fori_loop(0, n, step, 0)


def lanes(shape):
    return lax.broadcasted_iota(jnp.int32, shape, 1)


class Halo:
    def __init__(self, stack, packed, edges, ssem, rsem):
        self.stack, self.edges, self.packed = stack, edges, packed
        self.sems = ssem, rsem
        r, c = position()
        up, down, left, right = r > 0, r < 15, c > 0, c < 7
        both = jnp.logical_and
        self.moves = [
            (stack.at[1, pl.ds(R + D, D)], stack.at[1, pl.ds(D, D)], 1, 0, down, up),
            (stack.at[1, pl.ds(2 * D, D)], stack.at[1, pl.ds(R + 2 * D, D)], -1, 0, up, down),
            (packed.at[1], edges.at[0, pl.ds(1, 4)], 0, 1, right, left),
            (packed.at[0], edges.at[1, pl.ds(1, 4)], 0, -1, left, right),
            (packed.at[1, 3], edges.at[0, 0], 1, 1, both(down, right), both(up, left)),
            (packed.at[0, 3], edges.at[1, 0], 1, -1, both(down, left), both(up, right)),
            (packed.at[1, 0], edges.at[0, 5], -1, 1, both(up, right), both(down, left)),
            (packed.at[0, 0], edges.at[1, 5], -1, -1, both(up, left), both(down, right)),
        ]

    def copy(self, k):
        r, c = position()
        source, target, dr, dc, _, _ = self.moves[k]
        ssem, rsem = self.sems
        return pltpu.make_async_remote_copy(
            source, target, ssem.at[k], rsem.at[k],
            device_id=(jnp.clip(r + dr, 0, 15), jnp.clip(c + dc, 0, 7)), device_id_type=MESH)

    def start(self):
        for k in range(8):
            pl.when(self.moves[k][4])(lambda: self.copy(k).start())

    def arrived(self):
        for k in range(8):
            pl.when(self.moves[k][5])(lambda: self.copy(k).wait_recv())

    def sent(self):
        for k in range(8):
            pl.when(self.moves[k][4])(lambda: self.copy(k).wait_send())

    def clear(self):
        stack, edges = self.stack, self.edges
        r, c = position()
        zero_rows = jnp.zeros((D, C, W), BF16)
        zero_corner = jnp.zeros((C, W), BF16)
        zero_cols = jnp.zeros(edges.shape[1:], BF16)

        @pl.when(r == 0)
        def _():
            stack[1, D : 2 * D] = zero_rows
            edges[0, 0] = zero_corner
            edges[1, 0] = zero_corner

        @pl.when(r == 15)
        def _():
            stack[1, R + 2 * D : R + 3 * D] = zero_rows
            edges[0, 5] = zero_corner
            edges[1, 5] = zero_corner

        @pl.when(c == 0)
        def _():
            edges[0] = zero_cols

        @pl.when(c == 7)
        def _():
            edges[1] = zero_cols

    def pack(self):
        stack, packed = self.stack, self.packed
        lane = lanes((C, W))

        def group(g):
            first = jnp.zeros((C, W), F32)
            last = jnp.zeros((C, W), F32)
            for k in range(16):
                v = stack[1, 16 * g + k + 16].astype(F32)
                mine = jnp.logical_and(lane >= 8 * k, lane < 8 * k + 8)
                first = jnp.where(mine, pltpu.roll(v, 8 * k, 1) if k else v, first)
                last = jnp.where(mine, pltpu.roll(v, (8 * k + 8) % W, 1) if k < 15 else v, last)
            packed[0, g] = first.astype(BF16)
            packed[1, g] = last.astype(BF16)

        loop(4, group)

    def shift(self):
        stack, edges = self.stack, self.edges
        lane = lanes((C, W))

        def eight(g, half):
            before = edges[0, g].astype(F32)
            after = edges[1, g].astype(F32)
            for k in range(8 * half, 8 * half + 8):
                v = stack[1, 16 * g + k].astype(F32)
                b = pltpu.roll(before, (W - 8 * k) % W, 1) if k else before
                a = pltpu.roll(after, (W - 8 - 8 * k) % W, 1) if k < 15 else after
                stack[0, 16 * g + k] = jnp.where(lane < D, b, pltpu.roll(v, D, 1)).astype(BF16)
                stack[2, 16 * g + k] = jnp.where(lane >= W - D, a, pltpu.roll(v, W - D, 1)).astype(BF16)

        def group(i):
            eight(i, 1)
            eight(i + 1, 0)

        loop(5, group)


def tap_rows(stack, row, count):
    parts = []
    for p in range(3):
        for q in range(3):
            parts.append(jnp.concatenate([stack[q, row + D + D * p + k] for k in range(count)], axis=1))
    return jnp.concatenate(parts, axis=0)


def split_pair(a, b, i, kept, sent):
    core = lax.rem(position()[0], 2)
    lane = lanes((R, W))
    low = jnp.where(lane < 64, a, pltpu.roll(b, 64, 1)).astype(BF16)
    high = jnp.where(lane < 64, pltpu.roll(a, 64, 1), b).astype(BF16)
    is_low = core == 0
    kept[i, core] = jnp.where(is_low, low, high)
    sent[i] = jnp.where(is_low, high, low)


class CoreExchange:
    def __init__(self, sent, kept, ssem, rsem):
        self.refs = sent, kept, ssem, rsem

    def copy(self, k, core):
        sent, kept, ssem, rsem = self.refs
        r, c = position()
        part = pl.ds(8 * k, 8)
        return pltpu.make_async_remote_copy(
            sent.at[part], kept.at[part, core], ssem.at[k], rsem.at[k],
            device_id=(r + 1 - 2 * lax.rem(r, 2), c), device_id_type=MESH)

    def start(self, k):
        self.copy(k, lax.rem(position()[0], 2)).start()

    def arrived(self, k):
        self.copy(k, 1 - lax.rem(position()[0], 2)).wait_recv()

    def sent(self):
        loop(4, lambda k: self.copy(k, lax.rem(position()[0], 2)).wait_send())


def flip_out(exchange, kept, stops, sems):
    def part(k):
        exchange.arrived(k)

        def two(n):
            for mode in range(2):
                i = 2 * n + mode
                block = kept[i].reshape(2 * R, W)
                stops[0][i] = jnp.transpose(block, (1, 0)).reshape(2, R, W)
                relay_start(stops, 0, (mode, n), sems)

        loop(4, lambda m: two(4 * k + m))

    loop(4, part)


def others(n, me, body):
    def one(k):
        @pl.when(k != me)
        def _():
            body(k)

    loop(n, one)


def kernel(x_ref, cot_ref, w_ref, bias_ref, sym_ref, gin_ref, gw_ref, gb_ref,
           x_in, cot_in, wf, wb, bias2, flat, xs, gs, gzero, slope, mixed, xpack, xedge, gpack, gedge,
           csend, ckeep, c0, c1, c2, c3, msend, mkeep, m0, m1, m2, m3,
           gsum, gall, rs_in, rs_mine, ar_in, ag,
           in_sem, cc_ssem, cc_rsem, mc_ssem, mc_rsem, xh_ssem, xh_rsem, gh_ssem, gh_rsem,
           c_ssem, c_rsem, m_ssem, m_rsem, rs_ssem, rs_rsem, ar_ssem, ar_rsem, ag_ssem, ag_rsem):
    r, c = position()
    barrier = pltpu.get_barrier_semaphore()
    loop(128, lambda i: pl.semaphore_signal(
        barrier, 1, device_id=(lax.div(i, 8), lax.rem(i, 8)), device_id_type=MESH))
    x_copy = pltpu.make_async_copy(x_ref, x_in, in_sem.at[0])
    cot_copy = pltpu.make_async_copy(cot_ref, cot_in, in_sem.at[1])
    cot_copy.start()
    x_copy.start()

    cstops, mstops = (c0, c1, c2, c3), (m0, m1, m2, m3)
    csems, msems = (c_ssem, c_rsem), (m_ssem, m_rsem)
    cot_cores = CoreExchange(csend, ckeep, cc_ssem, cc_rsem)
    mix_cores = CoreExchange(msend, mkeep, mc_ssem, mc_rsem)
    xhalo = Halo(xs, xpack, xedge, xh_ssem, xh_rsem)
    ghalo = Halo(gs, gpack, gedge, gh_ssem, gh_rsem)

    spot = lax.broadcasted_iota(jnp.int32, (C, W), 0)
    left = (spot == lanes((C, W))).astype(BF16)
    right = (spot + C == lanes((C, W))).astype(BF16)
    for t in range(0, 9, 2):
        for out, at, dims in ((wf, lambda t: (t // 3, t % 3), ((1,), (0,))),
                              (wb, lambda t: (2 - t // 3, 2 - t % 3), ((0,), (0,)))):
            value = lax.dot_general(w_ref[at(t)], left, (dims, ((), ())), preferred_element_type=F32)
            if t < 8:
                value += lax.dot_general(w_ref[at(t + 1)], right, (dims, ((), ())), preferred_element_type=F32)
            out[:, C * t : C * t + W] = value.astype(BF16)
    bias2[...] = jnp.transpose(jnp.broadcast_to(bias_ref[...], (W, C)), (1, 0))

    xhalo.clear()
    ghalo.clear()
    gzero[0:16] = jnp.zeros((16, C, W), BF16)
    gzero[80:96] = jnp.zeros((16, C, W), BF16)
    cot_copy.wait()
    loop(PIECES, lambda i: split_pair(cot_in[i].astype(F32), cot_in[i + PIECES].astype(F32), i, ckeep, csend))
    x_copy.wait()

    def widen(i):
        flat[pl.ds(pl.multiple_of(i * R, R), R), :] = x_in[i].astype(F32)

    loop(C, widen)

    def to_row(i):
        xs[1, i + 16] = flat[pl.ds(i, C, stride=R), :].astype(BF16)

    loop(R, to_row)
    xhalo.pack()
    pl.semaphore_wait(barrier, 128)
    loop(4, cot_cores.start)
    xhalo.start()
    flip_out(cot_cores, ckeep, cstops, csems)
    xhalo.arrived()
    xhalo.shift()
    wide_bias = jnp.concatenate([bias2[...]] * 4, axis=1)

    def forward(i):
        row = 4 * i
        pre = jnp.dot(wf[:, 0 : 9 * C], tap_rows(xs, row, 4), preferred_element_type=F32) + wide_bias
        e = jnp.exp(jnp.minimum(pre, 0.0))
        up = pre > 0
        act = jnp.where(up, pre, e - 1.0)
        slp = jnp.where(up, 1.0, e)
        for k in range(4):
            at = slice(k * W, (k + 1) * W)
            value = xs[1, row + k + 16].astype(F32) + act[:, at]
            flat[pl.ds(row + k, C, stride=R), :] = value
            slope[row + k] = slp[:, at]
        pass_on(cstops, 0, i, csems)

    loop(R // 4, forward)

    def split_mixed(n):
        for mode in range(2):
            i = 2 * n + mode
            a = flat[pl.ds(pl.multiple_of(i * R, R), R), :]
            b = flat[pl.ds(pl.multiple_of((i + PIECES) * R, R), R), :]
            mixed[i] = a.astype(BF16)
            mixed[i + PIECES] = b.astype(BF16)
            split_pair(a, b, i, mkeep, msend)

    def mix_part(k):
        loop(4, lambda m: split_mixed(4 * k + m))
        mix_cores.start(k)
        loop(4, lambda m: pass_on(cstops, 1, 4 * k + m, csems))

    loop(4, mix_part)
    flip_out(mix_cores, mkeep, mstops, msems)

    def grad_mixed(n):
        for mode in range(2):
            i = 2 * n + mode
            relay_arrived(cstops, 2, (mode, n), csems)
            for h in range(2):
                ch = i + PIECES * h
                flat[pl.ds(pl.multiple_of(ch * R, R), R), :] = (
                    cot_in[ch].astype(F32) + c3[i, h].astype(F32))

    loop(PIECES // 2, grad_mixed)

    def grad_pre(i, total):
        g = (flat[pl.ds(i, C, stride=R), :] * slope[i]).astype(BF16)
        gs[1, i + 16] = g
        gzero[i + 16] = g
        return total + g.astype(F32)

    bias_total = lax.fori_loop(0, R, grad_pre, jnp.zeros((C, W), F32))
    ghalo.pack()
    ghalo.start()

    def weight_step(i):
        at = 8 + 4 * i
        g = jnp.concatenate([
            jnp.concatenate([gzero[at + k + D - D * p] for k in range(4)], axis=1) for p in range(3)], axis=0)
        v = jnp.concatenate([
            jnp.concatenate([xs[q, at + k] for k in range(4)], axis=1) for q in range(3)], axis=0)
        gsum[:, 0 : 3 * C] += lax.dot_general(g, v, (((1,), (1,)), ((), ())), preferred_element_type=F32)

    gsum[...] = jnp.zeros(gsum.shape, F32)
    loop(20, weight_step)
    lane = lanes((C, W))
    gsum[0:C, W : 2 * W] = jnp.where(
        lane < C, gsum[0:C, W : 2 * W], jnp.sum(bias_total, axis=1, keepdims=True))

    def piece(k):
        high, half = lax.div(k, 2), lax.rem(k, 2)
        return gsum.at[pl.ds(pl.multiple_of(high * 24, 8), 24), pl.ds(pl.multiple_of(half * W, W), W)]

    def rs_copy(k, slot, sem):
        return pltpu.make_async_remote_copy(
            piece(k), rs_in.at[slot], rs_ssem.at[k], rs_rsem.at[slot], device_id=(k, c), device_id_type=MESH)

    def ar_copy(k, slot):
        return pltpu.make_async_remote_copy(
            rs_mine, ar_in.at[slot], ar_ssem.at[k], ar_rsem.at[slot], device_id=(r, k), device_id_type=MESH)

    def ag_copy(k, slot):
        return pltpu.make_async_remote_copy(
            ag.at[r], ag.at[slot], ag_ssem.at[k], ag_rsem.at[slot], device_id=(k, c), device_id_type=MESH)

    others(16, r, lambda k: rs_copy(k, r, None).start())
    loop(PIECES // 2, lambda n: pass_on(mstops, 0, n, msems))
    ghalo.arrived()
    ghalo.shift()
    rs_in[r] = piece(r)[...]
    others(16, r, lambda k: rs_copy(k, k, None).wait_recv())
    rs_mine[...] = jnp.sum(rs_in[...], axis=0)
    others(8, c, lambda k: ar_copy(k, c).start())

    def backward(i):
        row = 4 * i
        back = jnp.dot(wb[:, 0 : 9 * C], tap_rows(gs, row, 4), preferred_element_type=F32)
        for k in range(4):
            flat[pl.ds(row + k, C, stride=R), :] = back[:, k * W : (k + 1) * W]

    loop(8, backward)
    ar_in[c] = rs_mine[...]
    others(8, c, lambda k: ar_copy(k, k).wait_recv())
    ag[r] = jnp.sum(ar_in[...], axis=0) * (1.0 / 1024)
    others(16, r, lambda k: ag_copy(k, r).start())
    loop(PIECES // 2, lambda n: pass_on(mstops, 1, n, msems))
    loop(8, lambda i: backward(i + 8))

    def input_out(i):
        for h in range(2):
            ch = i + PIECES * h
            gm = cot_in[ch].astype(F32) + c3[i, h].astype(F32)
            gin_ref[ch] = (gm + flat[pl.ds(pl.multiple_of(ch * R, R), R), :]).astype(BF16)

    loop(PIECES, input_out)

    def drain(stops, s, sems):
        def two(n):
            for mode in range(2):
                relay_sent(stops, s, (mode, n), sems)

        loop(PIECES // 2, two)

    cot_cores.sent()
    mix_cores.sent()
    xhalo.sent()
    ghalo.sent()
    for s in range(3):
        drain(cstops, s, csems)
    for s in range(2):
        drain(mstops, s, msems)
    others(16, r, lambda k: rs_copy(k, r, None).wait_send())
    others(8, c, lambda k: ar_copy(k, c).wait_send())
    others(16, r, lambda k: ag_copy(k, k).wait_recv())
    for k in range(16):
        gall[24 * (k // 2) : 24 * (k // 2) + 24, W * (k % 2) : W * (k % 2) + W] = ag[k]
    for p in range(3):
        two = gall[C * p : C * p + C, 0:W]
        gw_ref[p, 0] = two[:, 0:C]
        gw_ref[p, 1] = pltpu.roll(two, C, 1)[:, 0:C]
        gw_ref[p, 2] = gall[C * p : C * p + C, W : W + C]
    gb_ref[...] = jnp.transpose(gall[0:C, W : 2 * W], (1, 0))[C : C + 8, :]

    def sym_out(n):
        for mode in range(2):
            i = 2 * n + mode
            relay_arrived(mstops, 2, (mode, n), msems)
            for h in range(2):
                ch = i + PIECES * h
                sym_ref[ch] = (mixed[ch].astype(F32) + m3[i, h].astype(F32)).astype(BF16)

    loop(PIECES // 2, sym_out)
    drain(mstops, 2, msems)
    others(16, r, lambda k: ag_copy(k, r).wait_send())


def block(x, weight, bias, cot):
    vmem = pl.BlockSpec(memory_space=pltpu.VMEM)
    hbm = pl.BlockSpec(memory_space=pl.ANY)
    tile = pltpu.VMEM((C, R, W), BF16)
    stop = pltpu.VMEM((PIECES, 2, R, W), BF16)
    stack = pltpu.VMEM((3, R + 4 * D, C, W), BF16)
    pack, edge = pltpu.VMEM((2, 4, C, W), BF16), pltpu.VMEM((2, 6, C, W), BF16)
    weights = pltpu.VMEM((C, 640), BF16)
    dma = pltpu.SemaphoreType.DMA
    sym, gin, gw, gb = pl.pallas_call(
        kernel,
        out_shape=(
            jax.ShapeDtypeStruct((C, R, W), BF16),
            jax.ShapeDtypeStruct((C, R, W), BF16),
            jax.ShapeDtypeStruct((3, 3, C, C), F32),
            jax.ShapeDtypeStruct((8, C), F32),
        ),
        in_specs=[hbm, hbm, vmem, vmem],
        out_specs=[vmem] * 4,
        scratch_shapes=[
            tile, tile, weights, weights, pltpu.VMEM((C, W), F32),
            pltpu.VMEM((C * R, W), F32), stack, stack, pltpu.VMEM((R + 4 * D, C, W), BF16),
            pltpu.VMEM((R, C, W), F32), tile, pack, edge, pack, edge,
            pltpu.VMEM((PIECES, R, W), BF16), stop, stop, stop, stop, stop,
            pltpu.VMEM((PIECES, R, W), BF16), stop, stop, stop, stop, stop,
            pltpu.VMEM((3 * C, 2 * W), F32), pltpu.VMEM((3 * C, 2 * W), F32),
            pltpu.VMEM((16, 24, W), F32), pltpu.VMEM((24, W), F32),
            pltpu.VMEM((8, 24, W), F32), pltpu.VMEM((16, 24, W), F32),
            dma((2,)), dma((4,)), dma((4,)), dma((4,)), dma((4,)), dma((8,)), dma((8,)), dma((8,)), dma((8,)),
            dma((3, PIECES)), dma((3, PIECES)), dma((3, PIECES)), dma((3, PIECES)),
            dma((16,)), dma((16,)), dma((8,)), dma((8,)), dma((16,)), dma((16,)),
        ],
        compiler_params=pltpu.CompilerParams(
            collective_id=0, has_side_effects=True, vmem_limit_bytes=60 * 1024 * 1024),
    )(x, cot, weight, bias.reshape(1, C))
    return sym, gin, gw, gb[0]


def solution(mesh):
    tile = P(None, "row", "col")
    return jax.shard_map(
        block,
        mesh=mesh,
        in_specs=(tile, P(), P(), tile),
        out_specs=(tile, tile, P(), P()),
        check_vma=False,
    )
```

profile of v0, /device:TPU:1, one launch (start us, length us, event | category | flops | bytes accessed | tf_op | source)
XLA Modules:
  0.0 86.3 jit_solution(3102293457241583067)
XLA Ops:
  0.6 80.2 %shard_map.75 = (bf16[64,64,128]{2,1,0:T(8,128)(2,1)}, bf16[64,64,128]{2,1,0:T(8,128)(2,1)}, f32[3,3,64,64]{3,2,1,0:T(8,128)}, f32[8,64]{1,0:T(8,128)}) custom-call(bf16[64,64,128]{2,1,0:T(8,128)(2,1)} %x_ref.1, bf16[64,64,128]{2,1,0:T(8,128)(2,1)} %cot_ref.1, bf16[3,3,64,64]{3,2,1,0:T(8,128)(2,1)} %w_ref.1, f32[1,64]{1,0:T(1,128)} %bitcast.3), custom_call_target="tpu_custom_call" | custom-call | tf_op jit(solution)/shard_map/pallas_call | solution.py:506
  80.9 1.2 %slice_bitcast_fusion = f32[64]{0:T(128)} fusion(f32[8,64]{1,0:T(8,128)} %get-tuple-element.11), kind=kLoop, calls=%fused_computation | loop fusion | bytes 512 | tf_op jit(solution)/shard_map/squeeze | solution.py:532
  82.1 0.0 copy-start
  82.1 2.4 %copy.11 = bf16[64,64,128]{2,1,0:T(8,128)(2,1)} copy(bf16[64,64,128]{2,1,0:T(8,128)(2,1)} %get-tuple-element.16) | data formatting | bytes 2097152
  84.4 0.0 copy-done
  84.4 0.0 copy-start.1
  84.4 1.0 %copy.12 = bf16[64,64,128]{2,1,0:T(8,128)(2,1)} copy(bf16[64,64,128]{2,1,0:T(8,128)(2,1)S(1)} %copy-done) | data formatting | bytes 2097152
  85.4 0.2 copy-done.1
  85.6 0.7 copy.13
Async XLA Ops:
  82.1 2.4 %copy-start = (bf16[64,64,128]{2,1,0:T(8,128)(2,1)S(1)}, bf16[64,64,128]{2,1,0:T(8,128)(2,1)}, u32[]{:S(2)}) copy-start(bf16[64,64,128]{2,1,0:T(8,128)(2,1)} %get-tuple-element.17) | copy-start | bytes 3145732
  84.4 1.1 %copy-start.1 = (f32[3,3,64,64]{3,2,1,0:T(8,128)S(1)}, f32[3,3,64,64]{3,2,1,0:T(8,128)}, u32[]{:S(2)}) copy-start(f32[3,3,64,64]{3,2,1,0:T(8,128)} %get-tuple-element.18) | copy-start | bytes 442372
where the time goes:
time: 86.6 us; the launch traced here: 86.3 us
  Pallas kernels  80.2 us (93%)
  local copies, waits for them, and re-layouts  5.39 us (6%)
    pallas_call x1, Pallas kernels, block(): pl.pallas_call(kernel, out_shape=(jax.ShapeDtypeStruct((C, R, W), BF16),...  80.2 us
    unnamed x7, local copies, waits for them, and re-layouts  4.19 us

commit v1 on v0

--- a/solution.py
+++ b/solution.py
@@ -40,7 +40,8 @@
     chip_row, core = lax.div(r, 2), lax.rem(r, 2)
     x, z = mod4(chip_row), mod4(c)
     y = 2 * lax.div(chip_row, 4) + lax.div(c, 4)
-    j, how = mod4(n), lax.div(n, 4)
+    k, how = lax.div(n, 4), lax.rem(n, 4)
+    j = 2 * lax.rem(k, 2) + lax.div(k, 2)
     u, v = (z, x) if mode else (x, z)
     if stage == 0:
         u = mod4(u + v + j)
@@ -56,41 +57,44 @@
     return nr, nc, jnp.logical_and(nr == r, nc == c)
 
 
-def relay_copy(stops, s, p, sems):
+def relay_copies(stops, s, p, sems):
     nr, nc, here = next_stop(s, p)
+    r, _ = position()
+    core = lax.rem(r, 2)
     mode, n = p
     i = 2 * n + mode
     ssem, rsem = sems
-    remote = lambda: pltpu.make_async_remote_copy(
-        stops[s].at[i], stops[s + 1].at[i], ssem.at[s, i], rsem.at[s, i],
-        device_id=(nr, nc), device_id_type=MESH)
-    local = lambda: pltpu.make_async_copy(stops[s].at[i], stops[s + 1].at[i], rsem.at[s, i])
-    return remote, local, here
+
+    def message(source, target, send, receive, row, there):
+        remote = lambda: pltpu.make_async_remote_copy(
+            source, target, ssem.at[send, i], rsem.at[receive, i], device_id=(row, nc), device_id_type=MESH)
+        local = lambda: pltpu.make_async_copy(source, target, rsem.at[receive, i])
+        return remote, local, there
+
+    if s < 2:
+        return [message(stops[s].at[i], stops[s + 1].at[i], s, s, nr, here)]
+    return [message(stops[2].at[i, h], stops[3].at[i, core], 2 + h, 2 + core, nr - core + h,
+                    jnp.logical_and(here, core == h)) for h in range(2)]
 
 
 def relay_start(stops, s, p, sems):
-    remote, local, here = relay_copy(stops, s, p, sems)
-
-    @pl.when(here)
-    def _():
-        local().start()
-
-    @pl.when(jnp.logical_not(here))
-    def _():
-        remote().start()
+    for remote, local, here in relay_copies(stops, s, p, sems):
+        pl.when(here)(lambda: local().start())
+        pl.when(jnp.logical_not(here))(lambda: remote().start())
 
 
 def relay_arrived(stops, s, p, sems):
     i = 2 * p[1] + p[0]
-    pltpu.make_async_copy(stops[s].at[i], stops[s + 1].at[i], sems[1].at[s, i]).wait()
+    if s < 2:
+        pltpu.make_async_copy(stops[s].at[i], stops[s + 1].at[i], sems[1].at[s, i]).wait()
+    else:
+        for core in range(2):
+            pltpu.make_async_copy(stops[2].at[i, core], stops[3].at[i, core], sems[1].at[2 + core, i]).wait()
 
 
 def relay_sent(stops, s, p, sems):
-    remote, _, here = relay_copy(stops, s, p, sems)
-
-    @pl.when(jnp.logical_not(here))
-    def _():
-        remote().wait_send()
+    for remote, _, here in relay_copies(stops, s, p, sems):
+        pl.when(jnp.logical_not(here))(lambda: remote().wait_send())
 
 
 def pass_on(stops, s, n, sems):
@@ -99,12 +103,13 @@
         relay_start(stops, s + 1, (mode, n), sems)
 
 
-def loop(n, body):
+def loop(n, body, by=1):
     def step(i, carry):
-        body(i)
+        for k in range(by):
+            body(by * i + k)
         return carry
 
-    lax.fori_loop(0, n, step, 0)
+    lax.fori_loop(0, n // by, step, 0)
 
 
 def lanes(shape):
@@ -141,8 +146,8 @@
         for k in range(8):
             pl.when(self.moves[k][4])(lambda: self.copy(k).start())
 
-    def arrived(self):
-        for k in range(8):
+    def arrived(self, which):
+        for k in which:
             pl.when(self.moves[k][5])(lambda: self.copy(k).wait_recv())
 
     def sent(self):
@@ -193,7 +198,15 @@
 
         loop(4, group)
 
-    def shift(self):
+    def columns_in(self):
+        self.arrived((2, 3))
+        self.shift(True)
+
+    def rows_in(self):
+        self.arrived((0, 1, 4, 5, 6, 7))
+        self.shift(False)
+
+    def shift(self, own):
         stack, edges = self.stack, self.edges
         lane = lanes((C, W))
 
@@ -208,10 +221,14 @@
                 stack[2, 16 * g + k] = jnp.where(lane >= W - D, a, pltpu.roll(v, W - D, 1)).astype(BF16)
 
         def group(i):
-            eight(i, 1)
             eight(i + 1, 0)
-
-        loop(5, group)
+            eight(i + 1, 1)
+
+        if own:
+            loop(4, group)
+        else:
+            eight(0, 1)
+            eight(5, 0)
 
 
 def tap_rows(stack, row, count):
@@ -222,52 +239,14 @@
     return jnp.concatenate(parts, axis=0)
 
 
-def split_pair(a, b, i, kept, sent):
-    core = lax.rem(position()[0], 2)
+def flip(a, b):
+    return jnp.transpose(jnp.concatenate([a, b], axis=0), (1, 0)).reshape(2, R, W)
+
+
+def unfold(stop, i):
     lane = lanes((R, W))
-    low = jnp.where(lane < 64, a, pltpu.roll(b, 64, 1)).astype(BF16)
-    high = jnp.where(lane < 64, pltpu.roll(a, 64, 1), b).astype(BF16)
-    is_low = core == 0
-    kept[i, core] = jnp.where(is_low, low, high)
-    sent[i] = jnp.where(is_low, high, low)
-
-
-class CoreExchange:
-    def __init__(self, sent, kept, ssem, rsem):
-        self.refs = sent, kept, ssem, rsem
-
-    def copy(self, k, core):
-        sent, kept, ssem, rsem = self.refs
-        r, c = position()
-        part = pl.ds(8 * k, 8)
-        return pltpu.make_async_remote_copy(
-            sent.at[part], kept.at[part, core], ssem.at[k], rsem.at[k],
-            device_id=(r + 1 - 2 * lax.rem(r, 2), c), device_id_type=MESH)
-
-    def start(self, k):
-        self.copy(k, lax.rem(position()[0], 2)).start()
-
-    def arrived(self, k):
-        self.copy(k, 1 - lax.rem(position()[0], 2)).wait_recv()
-
-    def sent(self):
-        loop(4, lambda k: self.copy(k, lax.rem(position()[0], 2)).wait_send())
-
-
-def flip_out(exchange, kept, stops, sems):
-    def part(k):
-        exchange.arrived(k)
-
-        def two(n):
-            for mode in range(2):
-                i = 2 * n + mode
-                block = kept[i].reshape(2 * R, W)
-                stops[0][i] = jnp.transpose(block, (1, 0)).reshape(2, R, W)
-                relay_start(stops, 0, (mode, n), sems)
-
-        loop(4, lambda m: two(4 * k + m))
-
-    loop(4, part)
+    upper, lower = stop[i, 0].astype(F32), stop[i, 1].astype(F32)
+    return (jnp.where(lane < C, upper, pltpu.roll(lower, C, 1)), jnp.where(lane < C, pltpu.roll(upper, C, 1), lower))
 
 
 def others(n, me, body):
@@ -281,14 +260,21 @@
 
 def kernel(x_ref, cot_ref, w_ref, bias_ref, sym_ref, gin_ref, gw_ref, gb_ref,
            x_in, cot_in, wf, wb, bias2, flat, xs, gs, gzero, slope, mixed, xpack, xedge, gpack, gedge,
-           csend, ckeep, c0, c1, c2, c3, msend, mkeep, m0, m1, m2, m3,
+           c0, c1, c2, c3, m0, m1, m2, m3,
            gsum, gall, rs_in, rs_mine, ar_in, ag,
-           in_sem, cc_ssem, cc_rsem, mc_ssem, mc_rsem, xh_ssem, xh_rsem, gh_ssem, gh_rsem,
+           in_sem, out_sem, xh_ssem, xh_rsem, gh_ssem, gh_rsem,
            c_ssem, c_rsem, m_ssem, m_rsem, rs_ssem, rs_rsem, ar_ssem, ar_rsem, ag_ssem, ag_rsem):
     r, c = position()
     barrier = pltpu.get_barrier_semaphore()
-    loop(128, lambda i: pl.semaphore_signal(
-        barrier, 1, device_id=(lax.div(i, 8), lax.rem(i, 8)), device_id_type=MESH))
+    greet = lambda nr, nc: pl.semaphore_signal(barrier, 1, device_id=(nr, nc), device_id_type=MESH)
+    loop(32, lambda i: greet(lax.rem(i, 16), lax.div(i, 16) * 4 + mod4(c)), 4)
+    own_half = mod4(lax.div(r, 2)) * 2 + lax.rem(r, 2)
+    for k in range(1, 4):
+        loop(4, lambda i: greet(lax.div(i, 2) * 8 + own_half, lax.rem(i, 2) * 4 + mod4(c + k)), 4)
+    corners = [(dr, dc, jnp.logical_and(r + dr >= 0, r + dr < 16) & jnp.logical_and(c + dc >= 0, c + dc < 8))
+               for dr in (-1, 1) for dc in (-1, 1)]
+    for dr, dc, there in corners:
+        pl.when(there)(lambda: greet(r + dr, c + dc))
     x_copy = pltpu.make_async_copy(x_ref, x_in, in_sem.at[0])
     cot_copy = pltpu.make_async_copy(cot_ref, cot_in, in_sem.at[1])
     cot_copy.start()
@@ -296,11 +282,39 @@
 
     cstops, mstops = (c0, c1, c2, c3), (m0, m1, m2, m3)
     csems, msems = (c_ssem, c_rsem), (m_ssem, m_rsem)
-    cot_cores = CoreExchange(csend, ckeep, cc_ssem, cc_rsem)
-    mix_cores = CoreExchange(msend, mkeep, mc_ssem, mc_rsem)
     xhalo = Halo(xs, xpack, xedge, xh_ssem, xh_rsem)
     ghalo = Halo(gs, gpack, gedge, gh_ssem, gh_rsem)
 
+    xhalo.clear()
+    ghalo.clear()
+    cot_copy.wait()
+
+    def flip_cot(i):
+        c0[i] = flip(cot_in[i], cot_in[i + PIECES])
+
+    loop(PIECES, flip_cot, 2)
+    x_copy.wait()
+
+    def widen(i):
+        flat[pl.ds(pl.multiple_of(i * R, R), R), :] = x_in[i].astype(F32)
+
+    loop(C, widen, 4)
+
+    def to_row(i):
+        xs[1, i + 16] = flat[pl.ds(i, C, stride=R), :].astype(BF16)
+
+    loop(R, to_row, 4)
+    xhalo.pack()
+    beside_r = 2 - (r == 0).astype(jnp.int32) - (r == 15).astype(jnp.int32)
+    beside_c = 2 - (c == 0).astype(jnp.int32) - (c == 7).astype(jnp.int32)
+    pl.semaphore_wait(barrier, 44 + beside_r * beside_c)
+    xhalo.start()
+
+    def cot_out(n):
+        for mode in range(2):
+            relay_start(cstops, 0, (mode, n), csems)
+
+    loop(PIECES // 2, cot_out)
     spot = lax.broadcasted_iota(jnp.int32, (C, W), 0)
     left = (spot == lanes((C, W))).astype(BF16)
     right = (spot + C == lanes((C, W))).astype(BF16)
@@ -313,30 +327,10 @@
             out[:, C * t : C * t + W] = value.astype(BF16)
     bias2[...] = jnp.transpose(jnp.broadcast_to(bias_ref[...], (W, C)), (1, 0))
 
-    xhalo.clear()
-    ghalo.clear()
     gzero[0:16] = jnp.zeros((16, C, W), BF16)
     gzero[80:96] = jnp.zeros((16, C, W), BF16)
-    cot_copy.wait()
-    loop(PIECES, lambda i: split_pair(cot_in[i].astype(F32), cot_in[i + PIECES].astype(F32), i, ckeep, csend))
-    x_copy.wait()
-
-    def widen(i):
-        flat[pl.ds(pl.multiple_of(i * R, R), R), :] = x_in[i].astype(F32)
-
-    loop(C, widen)
-
-    def to_row(i):
-        xs[1, i + 16] = flat[pl.ds(i, C, stride=R), :].astype(BF16)
-
-    loop(R, to_row)
-    xhalo.pack()
-    pl.semaphore_wait(barrier, 128)
-    loop(4, cot_cores.start)
-    xhalo.start()
-    flip_out(cot_cores, ckeep, cstops, csems)
-    xhalo.arrived()
-    xhalo.shift()
+    loop(8, lambda n: pass_on(cstops, 0, n, csems))
+    xhalo.columns_in()
     wide_bias = jnp.concatenate([bias2[...]] * 4, axis=1)
 
     def forward(i):
@@ -351,35 +345,43 @@
             value = xs[1, row + k + 16].astype(F32) + act[:, at]
             flat[pl.ds(row + k, C, stride=R), :] = value
             slope[row + k] = slp[:, at]
-        pass_on(cstops, 0, i, csems)
-
-    loop(R // 4, forward)
-
-    def split_mixed(n):
+
+    def forward_and_pass(m):
+        forward(m + 2)
+        pass_on(cstops, 0, m + 8, csems)
+
+    loop(8, forward_and_pass)
+    loop(4, lambda m: forward(m + 10))
+    xhalo.rows_in()
+    for i in (0, 1, 14, 15):
+        forward(i)
+
+    def flip_mixed(n):
         for mode in range(2):
             i = 2 * n + mode
-            a = flat[pl.ds(pl.multiple_of(i * R, R), R), :]
-            b = flat[pl.ds(pl.multiple_of((i + PIECES) * R, R), R), :]
-            mixed[i] = a.astype(BF16)
-            mixed[i + PIECES] = b.astype(BF16)
-            split_pair(a, b, i, mkeep, msend)
-
-    def mix_part(k):
-        loop(4, lambda m: split_mixed(4 * k + m))
-        mix_cores.start(k)
-        loop(4, lambda m: pass_on(cstops, 1, 4 * k + m, csems))
-
-    loop(4, mix_part)
-    flip_out(mix_cores, mkeep, mstops, msems)
+            a = flat[pl.ds(pl.multiple_of(i * R, R), R), :].astype(BF16)
+            b = flat[pl.ds(pl.multiple_of((i + PIECES) * R, R), R), :].astype(BF16)
+            mixed[i] = a
+            mixed[i + PIECES] = b
+            m0[i] = flip(a, b)
+
+    def mix_out(n):
+        for mode in range(2):
+            relay_start(mstops, 0, (mode, n), msems)
+
+    loop(PIECES // 2, flip_mixed)
+    loop(8, lambda n: pass_on(cstops, 1, n, csems))
+    loop(8, lambda n: pass_on(cstops, 1, n + 8, csems))
+    loop(PIECES // 2, mix_out)
 
     def grad_mixed(n):
         for mode in range(2):
             i = 2 * n + mode
             relay_arrived(cstops, 2, (mode, n), csems)
-            for h in range(2):
+            for h, flipped in enumerate(unfold(c3, i)):
                 ch = i + PIECES * h
-                flat[pl.ds(pl.multiple_of(ch * R, R), R), :] = (
-                    cot_in[ch].astype(F32) + c3[i, h].astype(F32))
+                flat[pl.ds(pl.multiple_of(ch * R, R), R), :] = cot_in[ch].astype(F32) + flipped
+                c3[i, h] = flipped.astype(BF16)
 
     loop(PIECES // 2, grad_mixed)
 
@@ -389,9 +391,10 @@
         gzero[i + 16] = g
         return total + g.astype(F32)
 
-    bias_total = lax.fori_loop(0, R, grad_pre, jnp.zeros((C, W), F32))
-    ghalo.pack()
-    ghalo.start()
+    bias_total = lax.fori_loop(
+        0, R // 4, lambda i, t: functools.reduce(lambda u, k: grad_pre(4 * i + k, u), range(4), t),
+        jnp.zeros((C, W), F32))
+    loop(8, lambda n: pass_on(mstops, 0, n, msems))
 
     def weight_step(i):
         at = 8 + 4 * i
@@ -402,7 +405,13 @@
         gsum[:, 0 : 3 * C] += lax.dot_general(g, v, (((1,), (1,)), ((), ())), preferred_element_type=F32)
 
     gsum[...] = jnp.zeros(gsum.shape, F32)
-    loop(20, weight_step)
+
+    def weight_and_pass(n):
+        weight_step(n)
+        pass_on(mstops, 0, n + 8, msems)
+
+    loop(8, weight_and_pass)
+    loop(12, lambda i: weight_step(i + 8))
     lane = lanes((C, W))
     gsum[0:C, W : 2 * W] = jnp.where(
         lane < C, gsum[0:C, W : 2 * W], jnp.sum(bias_total, axis=1, keepdims=True))
@@ -423,14 +432,26 @@
         return pltpu.make_async_remote_copy(
             ag.at[r], ag.at[slot], ag_ssem.at[k], ag_rsem.at[slot], device_id=(k, c), device_id_type=MESH)
 
+    def drain(stops, s, sems):
+        def two(n):
+            for mode in range(2):
+                relay_sent(stops, s, (mode, n), sems)
+
+        loop(PIECES // 2, two)
+
     others(16, r, lambda k: rs_copy(k, r, None).start())
-    loop(PIECES // 2, lambda n: pass_on(mstops, 0, n, msems))
-    ghalo.arrived()
-    ghalo.shift()
+    ghalo.pack()
+    ghalo.start()
+    loop(8, lambda n: pass_on(mstops, 1, n, msems))
+    xhalo.sent()
+    for s in range(3):
+        drain(cstops, s, csems)
     rs_in[r] = piece(r)[...]
     others(16, r, lambda k: rs_copy(k, k, None).wait_recv())
     rs_mine[...] = jnp.sum(rs_in[...], axis=0)
     others(8, c, lambda k: ar_copy(k, c).start())
+    loop(8, lambda n: pass_on(mstops, 1, n + 8, msems))
+    ghalo.columns_in()
 
     def backward(i):
         row = 4 * i
@@ -438,35 +459,28 @@
         for k in range(4):
             flat[pl.ds(row + k, C, stride=R), :] = back[:, k * W : (k + 1) * W]
 
-    loop(8, backward)
+    loop(4, lambda i: backward(i + 2))
     ar_in[c] = rs_mine[...]
     others(8, c, lambda k: ar_copy(k, k).wait_recv())
     ag[r] = jnp.sum(ar_in[...], axis=0) * (1.0 / 1024)
     others(16, r, lambda k: ag_copy(k, r).start())
-    loop(PIECES // 2, lambda n: pass_on(mstops, 1, n, msems))
-    loop(8, lambda i: backward(i + 8))
+
+    loop(8, lambda i: backward(i + 6))
+    ghalo.rows_in()
+    for i in (0, 1, 14, 15):
+        backward(i)
 
     def input_out(i):
         for h in range(2):
             ch = i + PIECES * h
             gm = cot_in[ch].astype(F32) + c3[i, h].astype(F32)
-            gin_ref[ch] = (gm + flat[pl.ds(pl.multiple_of(ch * R, R), R), :]).astype(BF16)
-
-    loop(PIECES, input_out)
-
-    def drain(stops, s, sems):
-        def two(n):
-            for mode in range(2):
-                relay_sent(stops, s, (mode, n), sems)
-
-        loop(PIECES // 2, two)
-
-    cot_cores.sent()
-    mix_cores.sent()
-    xhalo.sent()
+            x_in[ch] = (gm + flat[pl.ds(pl.multiple_of(ch * R, R), R), :]).astype(BF16)
+
+    loop(PIECES, input_out, 2)
+    gin_copy = pltpu.make_async_copy(x_in, gin_ref, in_sem.at[0])
+    gin_copy.start()
+
     ghalo.sent()
-    for s in range(3):
-        drain(cstops, s, csems)
     for s in range(2):
         drain(mstops, s, msems)
     others(16, r, lambda k: rs_copy(k, r, None).wait_send())
@@ -479,19 +493,59 @@
         gw_ref[p, 0] = two[:, 0:C]
         gw_ref[p, 1] = pltpu.roll(two, C, 1)[:, 0:C]
         gw_ref[p, 2] = gall[C * p : C * p + C, W : W + C]
-    gb_ref[...] = jnp.transpose(gall[0:C, W : 2 * W], (1, 0))[C : C + 8, :]
+    gb_ref[...] = jnp.transpose(gall[0:C, W : 2 * W], (1, 0))[C : C + 1, :]
 
     def sym_out(n):
         for mode in range(2):
             i = 2 * n + mode
             relay_arrived(mstops, 2, (mode, n), msems)
-            for h in range(2):
+            for h, flipped in enumerate(unfold(m3, i)):
                 ch = i + PIECES * h
-                sym_ref[ch] = (mixed[ch].astype(F32) + m3[i, h].astype(F32)).astype(BF16)
-
-    loop(PIECES // 2, sym_out)
+                mixed[ch] = (mixed[ch].astype(F32) + flipped).astype(BF16)
+
+    def sym_copy(k, h):
+        part = pl.ds(pl.multiple_of(8 * k + PIECES * h, 8), 8)
+        return pltpu.make_async_copy(mixed.at[part], sym_ref.at[part], out_sem.at[2 * k + h])
+
+    def sym_part(k):
+        loop(4, lambda m: sym_out(4 * k + m))
+        sym_copy(k, 0).start()
+        sym_copy(k, 1).start()
+
+    loop(4, sym_part)
     drain(mstops, 2, msems)
+    gin_copy.wait()
+    for k in range(4):
+        sym_copy(k, 0).wait()
+        sym_copy(k, 1).wait()
     others(16, r, lambda k: ag_copy(k, r).wait_send())
+
+
+def place_kernel(*refs):
+    n = (len(refs) - 2) // 3
+    sources, targets, rooms, (came, went) = refs[:n], refs[n : 2 * n], refs[2 * n : 3 * n], refs[3 * n :]
+    ins = [pltpu.make_async_copy(a, b, came.at[k]) for k, (a, b) in enumerate(zip(sources, rooms))]
+    outs = [pltpu.make_async_copy(a, b, went.at[k]) for k, (a, b) in enumerate(zip(rooms, targets))]
+    for copy in ins:
+        copy.start()
+    for arrived, copy in zip(ins, outs):
+        arrived.wait()
+        copy.start()
+    for copy in outs:
+        copy.wait()
+
+
+def place(*arrays):
+    hbm = pl.BlockSpec(memory_space=pl.ANY)
+    n = len(arrays)
+    return pl.pallas_call(
+        place_kernel,
+        out_shape=tuple(jax.ShapeDtypeStruct(a.shape, a.dtype) for a in arrays),
+        in_specs=[hbm] * n,
+        out_specs=(hbm,) * n,
+        scratch_shapes=[pltpu.VMEM(a.shape, a.dtype) for a in arrays] + [pltpu.SemaphoreType.DMA((n,))] * 2,
+        compiler_params=pltpu.CompilerParams(vmem_limit_bytes=60 * 1024 * 1024),
+    )(*arrays)
 
 
 def block(x, weight, bias, cot):
@@ -509,27 +563,27 @@
             jax.ShapeDtypeStruct((C, R, W), BF16),
             jax.ShapeDtypeStruct((C, R, W), BF16),
             jax.ShapeDtypeStruct((3, 3, C, C), F32),
-            jax.ShapeDtypeStruct((8, C), F32),
+            jax.ShapeDtypeStruct((1, C), F32),
         ),
         in_specs=[hbm, hbm, vmem, vmem],
-        out_specs=[vmem] * 4,
+        out_specs=[hbm, hbm, vmem, vmem],
         scratch_shapes=[
             tile, tile, weights, weights, pltpu.VMEM((C, W), F32),
             pltpu.VMEM((C * R, W), F32), stack, stack, pltpu.VMEM((R + 4 * D, C, W), BF16),
             pltpu.VMEM((R, C, W), F32), tile, pack, edge, pack, edge,
-            pltpu.VMEM((PIECES, R, W), BF16), stop, stop, stop, stop, stop,
-            pltpu.VMEM((PIECES, R, W), BF16), stop, stop, stop, stop, stop,
+            stop, stop, stop, stop, stop, stop, stop, stop,
             pltpu.VMEM((3 * C, 2 * W), F32), pltpu.VMEM((3 * C, 2 * W), F32),
             pltpu.VMEM((16, 24, W), F32), pltpu.VMEM((24, W), F32),
             pltpu.VMEM((8, 24, W), F32), pltpu.VMEM((16, 24, W), F32),
-            dma((2,)), dma((4,)), dma((4,)), dma((4,)), dma((4,)), dma((8,)), dma((8,)), dma((8,)), dma((8,)),
-            dma((3, PIECES)), dma((3, PIECES)), dma((3, PIECES)), dma((3, PIECES)),
+            dma((2,)), dma((8,)), dma((8,)), dma((8,)), dma((8,)), dma((8,)),
+            dma((4, PIECES)), dma((4, PIECES)), dma((4, PIECES)), dma((4, PIECES)),
             dma((16,)), dma((16,)), dma((8,)), dma((8,)), dma((16,)), dma((16,)),
         ],
         compiler_params=pltpu.CompilerParams(
             collective_id=0, has_side_effects=True, vmem_limit_bytes=60 * 1024 * 1024),
     )(x, cot, weight, bias.reshape(1, C))
-    return sym, gin, gw, gb[0]
+    sym, gin, gw, gb = place(sym, gin, gw, gb)
+    return sym, gin, gw, gb.reshape(C)
 
 
 def solution(mesh):

time: 86.6 us -> 77.5 us (0.89)
  local copies, waits for them, and re-layouts: 5.39 us -> 0 us
  Pallas kernels: 80.2 us -> 76.7 us
    pallas_call x1, Pallas kernels: 80.2 us -> 74 us  [block(): pl.pallas_call(kernel, out_shape=(jax.ShapeDtypeStruct((C, R, W), BF16),...]
    unnamed x7 -> x0, local copies, waits for them, and re-layouts: 4.19 us -> none
    pallas_call x0 -> x1, Pallas kernels: none -> 2.7 us  [place(): pl.pallas_call(place_kernel, out_shape=tuple((jax.ShapeDtypeStruct(a.shap...]
    squeeze x1 -> x0, local copies, waits for them, and re-layouts: 1.19 us -> none  [block(): return (sym, gin, gw, gb[0])]
where the time goes in v1:
time: 77.5 us; the launch traced here: 77.4 us
  Pallas kernels  76.7 us (99%)
    pallas_call x1, Pallas kernels, block(): pl.pallas_call(kernel, out_shape=(jax.ShapeDtypeStruct((C, R, W), BF16),...  74 us
    pallas_call x1, Pallas kernels, place(): pl.pallas_call(place_kernel, out_shape=tuple((jax.ShapeDtypeStruct(a.shap...  2.7 us

profile of v1, /device:TPU:1, one launch (start us, length us, event | category | flops | bytes accessed | tf_op | source)
XLA Modules:
  0.0 77.4 jit_solution(3306664284728775961)
XLA Ops:
  0.6 74.0 %shard_map.75 = (bf16[64,64,128]{2,1,0:T(8,128)(2,1)}, bf16[64,64,128]{2,1,0:T(8,128)(2,1)}, f32[3,3,64,64]{3,2,1,0:T(8,128)}, f32[1,64]{1,0:T(1,128)}) custom-call(bf16[64,64,128]{2,1,0:T(8,128)(2,1)} %x_ref.1, bf16[64,64,128]{2,1,0:T(8,128)(2,1)} %cot_ref.1, bf16[3,3,64,64]{3,2,1,0:T(8,128)(2,1)} %w_ref.1, f32[1,64]{1,0:T(1,128)} %bitcast.2), custom_call_target="tpu_custom_call" | custom-call | tf_op jit(solution)/shard_map/pallas_call | solution.py:560
  74.7 2.7 %shard_map.76 = (bf16[64,64,128]{2,1,0:T(8,128)(2,1)}, bf16[64,64,128]{2,1,0:T(8,128)(2,1)}, f32[3,3,64,64]{3,2,1,0:T(8,128)}, f32[1,64]{1,0:T(1,128)}) custom-call(bf16[64,64,128]{2,1,0:T(8,128)(2,1)} %get-tuple-element.12.refs_0_, bf16[64,64,128]{2,1,0:T(8,128)(2,1)} %get-tuple-element.13.refs_1_, f32[3,3,64,64]{3,2,1,0:T(8,128)} %get-tuple-element.14.refs_2_, ...), custom_call_target="tpu_custom_call" | custom-call | tf_op jit(solution)/shard_map/pallas_call | solution.py:541

commit v2 on v1

--- a/solution.py
+++ b/solution.py
@@ -40,9 +40,14 @@
     chip_row, core = lax.div(r, 2), lax.rem(r, 2)
     x, z = mod4(chip_row), mod4(c)
     y = 2 * lax.div(chip_row, 4) + lax.div(c, 4)
-    k, how = lax.div(n, 4), lax.rem(n, 4)
-    j = 2 * lax.rem(k, 2) + lax.div(k, 2)
     u, v = (z, x) if mode else (x, z)
+    around = swap_outer(y) if stage == 1 else y + 1 - 2 * lax.rem(y, 2)
+    if isinstance(n, int):
+        j, how = 2 * (n // 4 % 2) + n // 8, n % 4
+        ny = around if how == 3 else swap_middle(y) if how == stage else y
+    else:
+        j, how = 2 * lax.rem(lax.div(n, 4), 2) + lax.div(n, 8), lax.rem(n, 4)
+        ny = jnp.where(how == 3, around, jnp.where(how == stage, swap_middle(y), y))
     if stage == 0:
         u = mod4(u + v + j)
     elif stage == 1:
@@ -50,8 +55,6 @@
     else:
         u = mod4(u - v - j + 8)
     nx, nz = (v, u) if mode else (u, v)
-    around = swap_outer(y) if stage == 1 else y + 1 - 2 * lax.rem(y, 2)
-    ny = jnp.where(how == 3, around, jnp.where(how == stage, swap_middle(y), y))
     nr = lax.div(ny, 2) * 8 + nx * 2 + core
     nc = lax.rem(ny, 2) * 4 + nz
     return nr, nc, jnp.logical_and(nr == r, nc == c)
@@ -110,6 +113,11 @@
         return carry
 
     lax.fori_loop(0, n // by, step, 0)
+
+
+def each(numbers, body):
+    for n in numbers:
+        body(n)
 
 
 def lanes(shape):
@@ -250,18 +258,14 @@
 
 
 def others(n, me, body):
-    def one(k):
-        @pl.when(k != me)
-        def _():
-            body(k)
-
-    loop(n, one)
-
-
-def kernel(x_ref, cot_ref, w_ref, bias_ref, sym_ref, gin_ref, gw_ref, gb_ref,
+    for k in range(n):
+        pl.when(k != me)(functools.partial(body, k))
+
+
+def kernel(x_ref, cot_ref, w_ref, bias_ref, sym_ref, gin_ref, g_ref,
            x_in, cot_in, wf, wb, bias2, flat, xs, gs, gzero, slope, mixed, xpack, xedge, gpack, gedge,
            c0, c1, c2, c3, m0, m1, m2, m3,
-           gsum, gall, rs_in, rs_mine, ar_in, ag,
+           gsum, gall, rs_in, rs_mine, ar_in,
            in_sem, out_sem, xh_ssem, xh_rsem, gh_ssem, gh_rsem,
            c_ssem, c_rsem, m_ssem, m_rsem, rs_ssem, rs_rsem, ar_ssem, ar_rsem, ag_ssem, ag_rsem):
     r, c = position()
@@ -314,7 +318,7 @@
         for mode in range(2):
             relay_start(cstops, 0, (mode, n), csems)
 
-    loop(PIECES // 2, cot_out)
+    each(range(16), cot_out)
     spot = lax.broadcasted_iota(jnp.int32, (C, W), 0)
     left = (spot == lanes((C, W))).astype(BF16)
     right = (spot + C == lanes((C, W))).astype(BF16)
@@ -329,7 +333,7 @@
 
     gzero[0:16] = jnp.zeros((16, C, W), BF16)
     gzero[80:96] = jnp.zeros((16, C, W), BF16)
-    loop(8, lambda n: pass_on(cstops, 0, n, csems))
+    each(range(8), lambda n: pass_on(cstops, 0, n, csems))
     xhalo.columns_in()
     wide_bias = jnp.concatenate([bias2[...]] * 4, axis=1)
 
@@ -353,8 +357,11 @@
     loop(8, forward_and_pass)
     loop(4, lambda m: forward(m + 10))
     xhalo.rows_in()
-    for i in (0, 1, 14, 15):
+    for k, i in enumerate((0, 1, 14, 15)):
         forward(i)
+        pass_on(cstops, 1, 2 * k, csems)
+        pass_on(cstops, 1, 2 * k + 1, csems)
+    each(range(8, 16), lambda n: pass_on(cstops, 1, n, csems))
 
     def flip_mixed(n):
         for mode in range(2):
@@ -370,9 +377,7 @@
             relay_start(mstops, 0, (mode, n), msems)
 
     loop(PIECES // 2, flip_mixed)
-    loop(8, lambda n: pass_on(cstops, 1, n, csems))
-    loop(8, lambda n: pass_on(cstops, 1, n + 8, csems))
-    loop(PIECES // 2, mix_out)
+    each(range(16), mix_out)
 
     def grad_mixed(n):
         for mode in range(2):
@@ -394,7 +399,7 @@
     bias_total = lax.fori_loop(
         0, R // 4, lambda i, t: functools.reduce(lambda u, k: grad_pre(4 * i + k, u), range(4), t),
         jnp.zeros((C, W), F32))
-    loop(8, lambda n: pass_on(mstops, 0, n, msems))
+    each(range(16), lambda n: pass_on(mstops, 0, n, msems))
 
     def weight_step(i):
         at = 8 + 4 * i
@@ -406,51 +411,54 @@
 
     gsum[...] = jnp.zeros(gsum.shape, F32)
 
-    def weight_and_pass(n):
-        weight_step(n)
-        pass_on(mstops, 0, n + 8, msems)
-
-    loop(8, weight_and_pass)
-    loop(12, lambda i: weight_step(i + 8))
+    loop(20, weight_step)
     lane = lanes((C, W))
     gsum[0:C, W : 2 * W] = jnp.where(
         lane < C, gsum[0:C, W : 2 * W], jnp.sum(bias_total, axis=1, keepdims=True))
 
-    def piece(k):
-        high, half = lax.div(k, 2), lax.rem(k, 2)
-        return gsum.at[pl.ds(pl.multiple_of(high * 24, 8), 24), pl.ds(pl.multiple_of(half * W, W), W)]
-
-    def rs_copy(k, slot, sem):
+    def piece(k, whole=gsum):
+        if isinstance(k, int):
+            return whole.at[24 * (k // 2) : 24 * (k // 2) + 24, W * (k % 2) : W * (k % 2) + W]
+        return whole.at[pl.ds(pl.multiple_of(lax.div(k, 2) * 24, 8), 24), pl.ds(pl.multiple_of(lax.rem(k, 2) * W, W), W)]
+
+    high, low = lax.div(r, 8), lax.div(c, 4)
+    near, far = low * 8 + lax.rem(r, 8), high * 4 + mod4(c)
+
+    def near_id(k):
+        return high * 8 + k % 8, k // 8 * 4 + mod4(c)
+
+    def far_id(k):
+        return k // 4 * 8 + lax.rem(r, 8), low * 4 + k % 4
+
+    def rs_copy(k, slot):
         return pltpu.make_async_remote_copy(
-            piece(k), rs_in.at[slot], rs_ssem.at[k], rs_rsem.at[slot], device_id=(k, c), device_id_type=MESH)
+            piece(k), rs_in.at[slot], rs_ssem.at[k], rs_rsem.at[slot], device_id=near_id(k), device_id_type=MESH)
 
     def ar_copy(k, slot):
         return pltpu.make_async_remote_copy(
-            rs_mine, ar_in.at[slot], ar_ssem.at[k], ar_rsem.at[slot], device_id=(r, k), device_id_type=MESH)
+            rs_mine, ar_in.at[slot], ar_ssem.at[k], ar_rsem.at[slot], device_id=far_id(k), device_id_type=MESH)
 
     def ag_copy(k, slot):
         return pltpu.make_async_remote_copy(
-            ag.at[r], ag.at[slot], ag_ssem.at[k], ag_rsem.at[slot], device_id=(k, c), device_id_type=MESH)
+            piece(near, gall), piece(slot, gall), ag_ssem.at[k], ag_rsem.at[slot], device_id=near_id(k), device_id_type=MESH)
 
     def drain(stops, s, sems):
-        def two(n):
+        for n in range(PIECES // 2):
             for mode in range(2):
                 relay_sent(stops, s, (mode, n), sems)
 
-        loop(PIECES // 2, two)
-
-    others(16, r, lambda k: rs_copy(k, r, None).start())
+    others(16, near, lambda k: rs_copy(k, near).start())
     ghalo.pack()
     ghalo.start()
-    loop(8, lambda n: pass_on(mstops, 1, n, msems))
+    each(range(8), lambda n: pass_on(mstops, 1, n, msems))
     xhalo.sent()
     for s in range(3):
         drain(cstops, s, csems)
-    rs_in[r] = piece(r)[...]
-    others(16, r, lambda k: rs_copy(k, k, None).wait_recv())
+    rs_in[near] = piece(near)[...]
+    others(16, near, lambda k: rs_copy(k, k).wait_recv())
     rs_mine[...] = jnp.sum(rs_in[...], axis=0)
-    others(8, c, lambda k: ar_copy(k, c).start())
-    loop(8, lambda n: pass_on(mstops, 1, n + 8, msems))
+    others(8, far, lambda k: ar_copy(k, far).start())
+    each(range(8, 16), lambda n: pass_on(mstops, 1, n, msems))
     ghalo.columns_in()
 
     def backward(i):
@@ -459,13 +467,13 @@
         for k in range(4):
             flat[pl.ds(row + k, C, stride=R), :] = back[:, k * W : (k + 1) * W]
 
-    loop(4, lambda i: backward(i + 2))
-    ar_in[c] = rs_mine[...]
-    others(8, c, lambda k: ar_copy(k, k).wait_recv())
-    ag[r] = jnp.sum(ar_in[...], axis=0) * (1.0 / 1024)
-    others(16, r, lambda k: ag_copy(k, r).start())
-
-    loop(8, lambda i: backward(i + 6))
+    loop(8, lambda i: backward(i + 2))
+    ar_in[far] = rs_mine[...]
+    others(8, far, lambda k: ar_copy(k, k).wait_recv())
+    piece(near, gall)[...] = jnp.sum(ar_in[...], axis=0) * (1.0 / 1024)
+    others(16, near, lambda k: ag_copy(k, near).start())
+
+    loop(4, lambda i: backward(i + 10))
     ghalo.rows_in()
     for i in (0, 1, 14, 15):
         backward(i)
@@ -483,17 +491,8 @@
     ghalo.sent()
     for s in range(2):
         drain(mstops, s, msems)
-    others(16, r, lambda k: rs_copy(k, r, None).wait_send())
-    others(8, c, lambda k: ar_copy(k, c).wait_send())
-    others(16, r, lambda k: ag_copy(k, k).wait_recv())
-    for k in range(16):
-        gall[24 * (k // 2) : 24 * (k // 2) + 24, W * (k % 2) : W * (k % 2) + W] = ag[k]
-    for p in range(3):
-        two = gall[C * p : C * p + C, 0:W]
-        gw_ref[p, 0] = two[:, 0:C]
-        gw_ref[p, 1] = pltpu.roll(two, C, 1)[:, 0:C]
-        gw_ref[p, 2] = gall[C * p : C * p + C, W : W + C]
-    gb_ref[...] = jnp.transpose(gall[0:C, W : 2 * W], (1, 0))[C : C + 1, :]
+    others(16, near, lambda k: rs_copy(k, near).wait_send())
+    others(8, far, lambda k: ar_copy(k, far).wait_send())
 
     def sym_out(n):
         for mode in range(2):
@@ -514,20 +513,38 @@
 
     loop(4, sym_part)
     drain(mstops, 2, msems)
+    others(16, near, lambda k: ag_copy(k, k).wait_recv())
+    g_copy = pltpu.make_async_copy(gall, g_ref, in_sem.at[1])
+    g_copy.start()
     gin_copy.wait()
+    g_copy.wait()
     for k in range(4):
         sym_copy(k, 0).wait()
         sym_copy(k, 1).wait()
-    others(16, r, lambda k: ag_copy(k, r).wait_send())
-
-
-def place_kernel(*refs):
-    n = (len(refs) - 2) // 3
-    sources, targets, rooms, (came, went) = refs[:n], refs[n : 2 * n], refs[2 * n : 3 * n], refs[3 * n :]
-    ins = [pltpu.make_async_copy(a, b, came.at[k]) for k, (a, b) in enumerate(zip(sources, rooms))]
-    outs = [pltpu.make_async_copy(a, b, went.at[k]) for k, (a, b) in enumerate(zip(rooms, targets))]
+    others(16, near, lambda k: ag_copy(k, near).wait_send())
+
+
+def place_kernel(sym_ref, gin_ref, g_ref, sym_out, gin_out, gw_out, gb_out, sym, gin, grads, gw, came, went):
+    g_in = pltpu.make_async_copy(g_ref, grads, came.at[4])
+    g_in.start()
+    ins, outs = [], []
+    for k in range(2):
+        part = pl.ds(k * C // 2, C // 2)
+        for n, (a, b, room) in enumerate(((sym_ref, sym_out, sym), (gin_ref, gin_out, gin))):
+            ins.append(pltpu.make_async_copy(a.at[part], room.at[part], came.at[2 * k + n]))
+            outs.append(pltpu.make_async_copy(room.at[part], b.at[part], went.at[2 * k + n]))
     for copy in ins:
         copy.start()
+    g_in.wait()
+    for p in range(3):
+        two = grads[C * p : C * p + C, 0:W]
+        gw[p, 0] = two[:, 0:C]
+        gw[p, 1] = pltpu.roll(two, C, 1)[:, 0:C]
+        gw[p, 2] = grads[C * p : C * p + C, W : W + C]
+    gw_copy = pltpu.make_async_copy(gw, gw_out, went.at[4])
+    gw_copy.start()
+    outs.append(gw_copy)
+    gb_out[...] = jnp.transpose(grads[0:C, W : 2 * W], (1, 0))[C : C + 1, :]
     for arrived, copy in zip(ins, outs):
         arrived.wait()
         copy.start()
@@ -535,17 +552,25 @@
         copy.wait()
 
 
-def place(*arrays):
+def place(sym, gin, grads):
     hbm = pl.BlockSpec(memory_space=pl.ANY)
-    n = len(arrays)
+    vmem = pl.BlockSpec(memory_space=pltpu.VMEM)
+    tile = pltpu.VMEM((C, R, W), BF16)
     return pl.pallas_call(
         place_kernel,
-        out_shape=tuple(jax.ShapeDtypeStruct(a.shape, a.dtype) for a in arrays),
-        in_specs=[hbm] * n,
-        out_specs=(hbm,) * n,
-        scratch_shapes=[pltpu.VMEM(a.shape, a.dtype) for a in arrays] + [pltpu.SemaphoreType.DMA((n,))] * 2,
+        out_shape=(
+            jax.ShapeDtypeStruct((C, R, W), BF16),
+            jax.ShapeDtypeStruct((C, R, W), BF16),
+            jax.ShapeDtypeStruct((3, 3, C, C), F32),
+            jax.ShapeDtypeStruct((1, C), F32),
+        ),
+        in_specs=[hbm] * 3,
+        out_specs=(hbm, hbm, hbm, vmem),
+        scratch_shapes=[
+            tile, tile, pltpu.VMEM((3 * C, 2 * W), F32), pltpu.VMEM((3, 3, C, C), F32),
+            pltpu.SemaphoreType.DMA((5,)), pltpu.SemaphoreType.DMA((5,))],
         compiler_params=pltpu.CompilerParams(vmem_limit_bytes=60 * 1024 * 1024),
-    )(*arrays)
+    )(sym, gin, grads)
 
 
 def block(x, weight, bias, cot):
@@ -557,16 +582,15 @@
     pack, edge = pltpu.VMEM((2, 4, C, W), BF16), pltpu.VMEM((2, 6, C, W), BF16)
     weights = pltpu.VMEM((C, 640), BF16)
     dma = pltpu.SemaphoreType.DMA
-    sym, gin, gw, gb = pl.pallas_call(
+    sym, gin, grads = pl.pallas_call(
         kernel,
         out_shape=(
             jax.ShapeDtypeStruct((C, R, W), BF16),
             jax.ShapeDtypeStruct((C, R, W), BF16),
-            jax.ShapeDtypeStruct((3, 3, C, C), F32),
-            jax.ShapeDtypeStruct((1, C), F32),
+            jax.ShapeDtypeStruct((3 * C, 2 * W), F32),
         ),
         in_specs=[hbm, hbm, vmem, vmem],
-        out_specs=[hbm, hbm, vmem, vmem],
+        out_specs=[hbm] * 3,
         scratch_shapes=[
             tile, tile, weights, weights, pltpu.VMEM((C, W), F32),
             pltpu.VMEM((C * R, W), F32), stack, stack, pltpu.VMEM((R + 4 * D, C, W), BF16),
@@ -574,7 +598,7 @@
             stop, stop, stop, stop, stop, stop, stop, stop,
             pltpu.VMEM((3 * C, 2 * W), F32), pltpu.VMEM((3 * C, 2 * W), F32),
             pltpu.VMEM((16, 24, W), F32), pltpu.VMEM((24, W), F32),
-            pltpu.VMEM((8, 24, W), F32), pltpu.VMEM((16, 24, W), F32),
+            pltpu.VMEM((8, 24, W), F32),
             dma((2,)), dma((8,)), dma((8,)), dma((8,)), dma((8,)), dma((8,)),
             dma((4, PIECES)), dma((4, PIECES)), dma((4, PIECES)), dma((4, PIECES)),
             dma((16,)), dma((16,)), dma((8,)), dma((8,)), dma((16,)), dma((16,)),
@@ -582,7 +606,7 @@
         compiler_params=pltpu.CompilerParams(
             collective_id=0, has_side_effects=True, vmem_limit_bytes=60 * 1024 * 1024),
     )(x, cot, weight, bias.reshape(1, C))
-    sym, gin, gw, gb = place(sym, gin, gw, gb)
+    sym, gin, gw, gb = place(sym, gin, grads)
     return sym, gin, gw, gb.reshape(C)
 
 

time: 77.5 us -> 75 us (0.968)
  Pallas kernels: 76.7 us -> 74.1 us
    pallas_call x1, Pallas kernels: 74 us -> 71.1 us  [block(): pl.pallas_call(kernel, out_shape=(jax.ShapeDtypeStruct((C, R, W), BF16),...]
where the time goes in v2:
time: 75 us; the launch traced here: 74.8 us
  Pallas kernels  74.1 us (99%)
    pallas_call x1, Pallas kernels, block(): pl.pallas_call(kernel, out_shape=(jax.ShapeDtypeStruct((C, R, W), BF16),...  71.1 us
    pallas_call x1, Pallas kernels, place(): pl.pallas_call(place_kernel, out_shape=(jax.ShapeDtypeStruct((C, R, W), B...  3.06 us

profile of v2, /device:TPU:1, one launch (start us, length us, event | category | flops | bytes accessed | tf_op | source)
XLA Modules:
  0.0 74.8 jit_solution(6093797488067217404)
XLA Ops:
  0.6 71.1 %shard_map.75 = (bf16[64,64,128]{2,1,0:T(8,128)(2,1)}, bf16[64,64,128]{2,1,0:T(8,128)(2,1)}, f32[192,256]{1,0:T(8,128)}) custom-call(bf16[64,64,128]{2,1,0:T(8,128)(2,1)} %x_ref.1, bf16[64,64,128]{2,1,0:T(8,128)(2,1)} %cot_ref.1, bf16[3,3,64,64]{3,2,1,0:T(8,128)(2,1)} %w_ref.1, f32[1,64]{1,0:T(1,128)} %bitcast.2), custom_call_target="tpu_custom_call" | custom-call | tf_op jit(solution)/shard_map/pallas_call | solution.py:585
  71.7 3.1 %shard_map.76 = (bf16[64,64,128]{2,1,0:T(8,128)(2,1)}, bf16[64,64,128]{2,1,0:T(8,128)(2,1)}, f32[3,3,64,64]{3,2,1,0:T(8,128)}, f32[1,64]{1,0:T(1,128)}) custom-call(bf16[64,64,128]{2,1,0:T(8,128)(2,1)} %get-tuple-element.11.sym_ref, bf16[64,64,128]{2,1,0:T(8,128)(2,1)} %get-tuple-element.12.gin_ref, f32[192,256]{1,0:T(8,128)} %get-tuple-element.13.g_ref), custom_call_target="tpu_custom_call" | custom-call | tf_op jit(solution)/shard_map/pallas_call | solution.py:559

commit v3 on v2

--- a/solution.py
+++ b/solution.py
@@ -297,28 +297,29 @@
         c0[i] = flip(cot_in[i], cot_in[i + PIECES])
 
     loop(PIECES, flip_cot, 2)
-    x_copy.wait()
-
-    def widen(i):
-        flat[pl.ds(pl.multiple_of(i * R, R), R), :] = x_in[i].astype(F32)
-
-    loop(C, widen, 4)
-
-    def to_row(i):
-        xs[1, i + 16] = flat[pl.ds(i, C, stride=R), :].astype(BF16)
-
-    loop(R, to_row, 4)
-    xhalo.pack()
     beside_r = 2 - (r == 0).astype(jnp.int32) - (r == 15).astype(jnp.int32)
     beside_c = 2 - (c == 0).astype(jnp.int32) - (c == 7).astype(jnp.int32)
     pl.semaphore_wait(barrier, 44 + beside_r * beside_c)
-    xhalo.start()
-
     def cot_out(n):
         for mode in range(2):
             relay_start(cstops, 0, (mode, n), csems)
 
-    each(range(16), cot_out)
+    each(range(8), cot_out)
+    x_copy.wait()
+
+    def widen(i):
+        flat[pl.ds(pl.multiple_of(i * R, R), R), :] = x_in[i].astype(F32)
+
+    loop(C, widen, 4)
+
+    def to_row(i):
+        xs[1, i + 16] = flat[pl.ds(i, C, stride=R), :].astype(BF16)
+
+    loop(R, to_row, 4)
+    xhalo.pack()
+    xhalo.start()
+
+    each(range(8, 16), cot_out)
     spot = lax.broadcasted_iota(jnp.int32, (C, W), 0)
     left = (spot == lanes((C, W))).astype(BF16)
     right = (spot + C == lanes((C, W))).astype(BF16)
@@ -361,7 +362,6 @@
         forward(i)
         pass_on(cstops, 1, 2 * k, csems)
         pass_on(cstops, 1, 2 * k + 1, csems)
-    each(range(8, 16), lambda n: pass_on(cstops, 1, n, csems))
 
     def flip_mixed(n):
         for mode in range(2):
@@ -377,6 +377,7 @@
             relay_start(mstops, 0, (mode, n), msems)
 
     loop(PIECES // 2, flip_mixed)
+    each(range(8, 16), lambda n: pass_on(cstops, 1, n, csems))
     each(range(16), mix_out)
 
     def grad_mixed(n):

time: 75 us -> 72.5 us (0.967)
  Pallas kernels: 74.1 us -> 71.6 us
    pallas_call x1, Pallas kernels: 71.1 us -> 68.6 us  [block(): pl.pallas_call(kernel, out_shape=(jax.ShapeDtypeStruct((C, R, W), BF16),...]
where the time goes in v3:
time: 72.5 us; the launch traced here: 72.3 us
  Pallas kernels  71.6 us (99%)
    pallas_call x1, Pallas kernels, block(): pl.pallas_call(kernel, out_shape=(jax.ShapeDtypeStruct((C, R, W), BF16),...  68.6 us
    pallas_call x1, Pallas kernels, place(): pl.pallas_call(place_kernel, out_shape=(jax.ShapeDtypeStruct((C, R, W), B...  3.06 us

profile of v3, /device:TPU:1, one launch (start us, length us, event | category | flops | bytes accessed | tf_op | source)
XLA Modules:
  0.0 72.3 jit_solution(11906076596419190517)
XLA Ops:
  0.6 68.6 %shard_map.75 = (bf16[64,64,128]{2,1,0:T(8,128)(2,1)}, bf16[64,64,128]{2,1,0:T(8,128)(2,1)}, f32[192,256]{1,0:T(8,128)}) custom-call(bf16[64,64,128]{2,1,0:T(8,128)(2,1)} %x_ref.1, bf16[64,64,128]{2,1,0:T(8,128)(2,1)} %cot_ref.1, bf16[3,3,64,64]{3,2,1,0:T(8,128)(2,1)} %w_ref.1, f32[1,64]{1,0:T(1,128)} %bitcast.2), custom_call_target="tpu_custom_call" | custom-call | tf_op jit(solution)/shard_map/pallas_call | solution.py:586
  69.2 3.1 %shard_map.76 = (bf16[64,64,128]{2,1,0:T(8,128)(2,1)}, bf16[64,64,128]{2,1,0:T(8,128)(2,1)}, f32[3,3,64,64]{3,2,1,0:T(8,128)}, f32[1,64]{1,0:T(1,128)}) custom-call(bf16[64,64,128]{2,1,0:T(8,128)(2,1)} %get-tuple-element.11.sym_ref, bf16[64,64,128]{2,1,0:T(8,128)(2,1)} %get-tuple-element.12.gin_ref, f32[192,256]{1,0:T(8,128)} %get-tuple-element.13.g_ref), custom_call_target="tpu_custom_call" | custom-call | tf_op jit(solution)/shard_map/pallas_call | solution.py:560
